TPU v7x, 256 devices: a whole 4x4x8 slice. The times are simulated.
256 devices in a mesh: ia: 8 (over z), ja: 32 (over y, x, core).
Axes of the slice: x: 4, y: 4, z: 8, core: 2. Of those that a mesh axis runs over, the one named last changes fastest.
Arguments:
- pno_basis: bfloat16 [8, 64, 512, 128], P('ia', 'ja'), may hold values from -0.4375 to 0.4375
- domain_map: int32 [8, 64, 512], replicated, may hold values from 0 to 1023, as said below
- amplitudes: float32 [8, 64, 128, 128], P('ia', 'ja'), may hold values from -6 to 6
- exchange_ints: float32 [8, 64, 128, 128], P('ia', 'ja'), may hold values from -6 to 6
- pno_energy: float32 [8, 64, 128], P('ia', 'ja'), may hold values from 0.5 to 3
- row_energy: float32 [8], P('ia'), may hold values from -1.5 to -0.3
- column_energy: float32 [64], P('ja'), may hold values from -1.5 to -0.3
- coupling_rows: float32 [8, 8], P('ia'), may hold values from -0.6 to 0.6
- coupling_columns: float32 [64, 64], P(None, 'ja'), may hold values from -0.6 to 0.6
- row_neighbours: int32 [8, 64, 6], P('ia', 'ja'), may hold values from 0 to 7, as said below
- column_neighbours: int32 [8, 64, 24], P('ia', 'ja'), may hold values from 0 to 63, as said below
- row_counts: int32 [8, 64], P('ia', 'ja'), may hold values from 1 to 6
- column_counts: int32 [8, 64], P('ia', 'ja'), may hold values from 1 to 24
Outputs:
- new_amplitudes: float32 [8, 64, 128, 128], P('ia', 'ja')
- pair_energy: float32 [8, 64], P('ia', 'ja')
Inputs may be any that keep to these rules, and one draw needn't show every extreme that they name: `domain_map`: the 512 entries of one pair are distinct. `row_neighbours`: the 6 entries of a pair (i, j) are distinct and differ from i. `column_neighbours`: the 24 entries of a pair (i, j) are distinct and differ from j.
All inputs are finite; a program needn't handle non-finite values.
Results may differ from a plain program's by a relative error of at most 0.008.
Values may be sent and summed in bfloat16 or wider, within the bound.
No kernel may reach another device: no remote copies, remote signals or barrier semaphores. Data moves between devices by JAX's collectives and lax.ppermute only.
A program may use at most 64 MiB of HBM per device.

v0:
```python
import jax
import jax.numpy as jnp
from jax import lax
from jax.sharding import PartitionSpec as P

ITERS = 2
level_shift = 0.3


def sent_to_all(shard, axis):
    copies = jnp.broadcast_to(shard, (lax.axis_size(axis), *shard.shape))
    return lax.all_to_all(copies, axis, split_axis=0, concat_axis=0, tiled=True)


def in_order(parts, dim):
    parts = jnp.moveaxis(parts, 0, dim)
    dims = parts.shape
    return parts.reshape(*dims[:dim], dims[dim] * dims[dim + 1], *dims[dim + 2 :])


def gathered_copies(shard, axis, dim):
    parts = sent_to_all(shard, axis)
    return in_order(parts, dim)


def pair_intersections(packed):
    own_domain, own_basis, partner_domains, partner_bases = packed
    match = (own_domain[None, :, None] == partner_domains[:, None, :]).astype(jnp.bfloat16)
    picked = jnp.einsum(
        "suv,svb->sub", match, partner_bases, preferred_element_type=jnp.float32
    ).astype(jnp.bfloat16)
    return jnp.einsum("ua,sub->sab", own_basis, picked, preferred_element_type=jnp.float32).astype(
        jnp.bfloat16
    )


def local(
    pno_basis,
    domain_map,
    amplitudes,
    exchange_ints,
    pno_energy,
    row_energy,
    column_energy,
    coupling_rows,
    coupling_columns,
    row_neighbours,
    column_neighbours,
    row_counts,
    column_counts,
):
    pair_rows = pno_basis.shape[0]
    pair_columns = pno_basis.shape[1]
    domain_size = pno_basis.shape[2]
    width = amplitudes.shape[-1]
    total_rows = domain_map.shape[0]
    total_columns = domain_map.shape[1]
    own_pairs = pair_rows * pair_columns
    row_offset = lax.axis_index("ia") * pair_rows
    column_offset = lax.axis_index("ja") * pair_columns
    domain_rows = lax.dynamic_slice_in_dim(domain_map, row_offset, pair_rows, 0)
    domain_columns = lax.dynamic_slice_in_dim(domain_map, column_offset, pair_columns, 1)
    own_domain = lax.dynamic_slice_in_dim(domain_rows, column_offset, pair_columns, 1).reshape(
        own_pairs, domain_size
    )
    own_basis = pno_basis.reshape(own_pairs, domain_size, width)
    local_rows = jnp.arange(pair_rows, dtype=jnp.int32)[:, None, None]
    local_columns = jnp.arange(pair_columns, dtype=jnp.int32)[None, :, None]
    row_slots = (row_neighbours * pair_columns + local_columns).reshape(own_pairs, -1)
    column_slots = (local_rows * total_columns + column_neighbours).reshape(own_pairs, -1)
    row_live = (
        jnp.arange(row_neighbours.shape[2], dtype=jnp.int32)[None, None, :] < row_counts[:, :, None]
    )
    row_table = jnp.broadcast_to(coupling_rows[:, None, :], (pair_rows, pair_columns, total_rows))
    row_weight = jnp.where(row_live, jnp.take_along_axis(row_table, row_neighbours, axis=2), 0.0)
    column_live = (
        jnp.arange(column_neighbours.shape[2], dtype=jnp.int32)[None, None, :]
        < column_counts[:, :, None]
    )
    column_table = coupling_columns.T[None, :, :]
    column_weight = jnp.where(
        column_live, jnp.take_along_axis(column_table, column_neighbours, axis=2), 0.0
    )
    weights = jnp.concatenate(
        [row_weight.reshape(own_pairs, -1), column_weight.reshape(own_pairs, -1)], axis=1
    )
    partner_domains = jnp.concatenate(
        [
            domain_columns.reshape(total_rows * pair_columns, domain_size)[row_slots],
            domain_rows.reshape(pair_rows * total_columns, domain_size)[column_slots],
        ],
        axis=1,
    )

    def slot_pick(column_slab, row_slab):
        column_flat = column_slab.reshape(
            (column_slab.shape[0] * column_slab.shape[1],) + column_slab.shape[2:]
        )
        row_flat = row_slab.reshape((row_slab.shape[0] * row_slab.shape[1],) + row_slab.shape[2:])
        return jnp.concatenate([column_flat[row_slots], row_flat[column_slots]], axis=1)

    energy_gap = (
        pno_energy[:, :, :, None]
        + pno_energy[:, :, None, :]
        - row_energy[:, None, None, None]
        - column_energy[None, :, None, None]
    )
    column_bases = gathered_copies(pno_basis, "ia", 0)
    row_bases = lax.all_gather(pno_basis, "ja", axis=1, tiled=True)
    partner_bases = slot_pick(column_bases, row_bases)
    stored = lax.map(pair_intersections, (own_domain, own_basis, partner_domains, partner_bases))
    current = amplitudes
    for iteration in range(ITERS):
        rounded = current.astype(jnp.bfloat16)
        column_rounded = gathered_copies(rounded, "ia", 0)
        row_rounded = lax.all_gather(rounded, "ja", axis=1, tiled=True)
        intersection_wide = stored.astype(jnp.float32)
        halved = jnp.einsum(
            "psab,psbc->psac",
            intersection_wide,
            slot_pick(column_rounded, row_rounded).astype(jnp.float32),
        ).astype(jnp.bfloat16)
        projected = jnp.einsum("psac,psdc->psad", halved.astype(jnp.float32), intersection_wide)
        coupled = jnp.sum(weights[:, :, None, None] * projected, axis=1).reshape(
            pair_rows, pair_columns, width, width
        )
        residual = exchange_ints + energy_gap * current - coupled
        current = current - residual / (energy_gap + level_shift)
    pair_energy = jnp.sum(
        exchange_ints * (2.0 * current - jnp.swapaxes(current, 2, 3)), axis=(2, 3)
    )
    return (current, pair_energy)


def solution(mesh):
    in_specs = (
        P("ia", "ja", None, None),
        P(),
        P("ia", "ja", None, None),
        P("ia", "ja", None, None),
        P("ia", "ja", None),
        P("ia"),
        P("ja"),
        P("ia", None),
        P(None, "ja"),
        P("ia", "ja", None),
        P("ia", "ja", None),
        P("ia", "ja"),
        P("ia", "ja"),
    )
    out_specs = (P("ia", "ja", None, None), P("ia", "ja"))
    return jax.shard_map(local, mesh=mesh, in_specs=in_specs, out_specs=out_specs, check_vma=False)
```

profile of v0, /device:TPU:1, one launch (start us, length us, event | category | flops | bytes accessed | tf_op | source)
XLA Modules:
  0.0 222.9 jit_solution(1346246131528462927)
XLA Ops:
  7.2 0.0 all-gather.6.cloned.1.call-start
  7.2 1.6 bitcast_convert_fusion
  8.9 0.0 all-gather.4.cloned.1.call-start
  8.9 0.7 all-gather.4.cloned.1.call-update
  9.6 0.9 fusion.78
  10.6 0.1 broadcast_in_dim.72
  10.7 25.0 %all_to_all.15 = bf16[8,1,2,128,128]{4,3,2,1,0:T(8,128)(2,1)} all-to-all(bf16[8,1,2,128,128]{4,3,2,1,0:T(8,128)(2,1)S(1)} %broadcast_in_dim.72), channel_id=1, replica_groups=mesh['ia'=8,'ja'=32] {'ia'}, dimensions={0} | all-to-all | bytes 1048576 | tf_op jit(solution)/shard_map/all_to_all | solution.py:12
  35.7 1.7 broadcast_in_dim.43
  37.4 3.7 %all-to-all-start = ((bf16[8,1,2,512,128]{4,3,2,1,0:T(8,128)(2,1)}), bf16[8,1,2,512,128]{4,3,2,1,0:T(8,128)(2,1)S(1)}, u32[]{:S(2)}, u32[]{:S(2)}) async-start(bf16[8,1,2,512,128]{4,3,2,1,0:T(8,128)(2,1)} %broadcast_in_dim.43), calls=%async_computation | async-start | bytes 4194304 | tf_op jit(solution)/shard_map/all_to_all | solution.py:12
  41.2 0.0 all-gather.8.cloned.1.call-start
  41.3 0.1 reshape.281
  41.4 0.1 reshape.273
  41.5 0.6 gather_fusion
  42.1 0.6 reshape.272
  42.7 0.1 reshape.337
  42.8 0.7 gather_fusion.8
  43.5 0.6 reshape.336
  44.2 0.1 reshape.345
  44.2 1.1 gather_fusion.9
  45.3 0.6 reshape.344
  46.6 1.3 gather_fusion.1
  47.9 0.7 fusion.66
  48.6 0.7 fusion.67
  49.3 0.1 pad_maximum_fusion.1
  49.4 0.9 pad_add_fusion
  50.3 2.4 %gather_fusion.4 = bf16[12,128,128]{2,1,0:T(8,128)(2,1)} fusion(bf16[16,128,128]{2,1,0:T(8,128)(2,1)} %bitcast.136, s32[1024]{0:T(1024)S(1)} %pad_clamp_fusion.1), kind=kCustom, calls=%fused_computation.4 | custom fusion | bytes 786480 | tf_op jit(solution)/shard_map/gather | solution.py:100
  52.7 40.0 %all-to-all-done = bf16[8,1,2,512,128]{4,3,2,1,0:T(8,128)(2,1)S(1)} async-done(((bf16[8,1,2,512,128]{4,3,2,1,0:T(8,128)(2,1)}), bf16[8,1,2,512,128]{4,3,2,1,0:T(8,128)(2,1)S(1)}, u32[]{:S(2)}, u32[]{:S(2)}) %all-to-all-start) | async-done | bytes 2097184 | tf_op jit(solution)/shard_map/all_to_all | solution.py:12
  92.8 1.9 gather_fusion.2
  94.7 3.6 %gather_fusion.5 = bf16[48,128,128]{2,1,0:T(8,128)(2,1)} fusion(bf16[64,128,128]{2,1,0:T(8,128)(2,1)} %bitcast.140, s32[1024]{0:T(1024)S(1)} %pad_clamp_fusion), kind=kCustom, calls=%fused_computation.5 | custom fusion | bytes 3145920 | tf_op jit(solution)/shard_map/gather | solution.py:100
  98.3 24.7 %all-gather.4.cloned.1.call-done = bf16[1,64,512,128]{3,2,0,1:T(8,128)(2,1)} async-done(((bf16[1,2,512,128]{3,2,0,1:T(8,128)(2,1)}), bf16[1,64,512,128]{3,2,0,1:T(8,128)(2,1)}) %all-gather.4.cloned.1.call-update) | async-done | bytes 8388624 | tf_op jit(solution)/shard_map/all_gather | solution.py:109
  122.9 8.5 %gather_fusion.3 = bf16[48,512,128]{2,1,0:T(8,128)(2,1)} fusion(bf16[64,512,128]{2,1,0:T(8,128)(2,1)} %bitcast.135, s32[1024]{0:T(1024)S(1)} %pad_clamp_fusion), kind=kCustom, calls=%fused_computation.3 | custom fusion | bytes 12583104 | tf_op jit(solution)/shard_map/gather | solution.py:100
  131.5 6.5 %pad_maximum_fusion = bf16[2,30,512,128]{3,2,1,0:T(8,128)(2,1)} fusion(bf16[2,24,512,128]{3,2,1,0:T(8,128)(2,1)} %bitcast.132, bf16[2,6,512,128]{3,2,1,0:T(8,128)(2,1)S(1)} %bitcast.134), kind=kLoop, calls=%fused_computation.26 | loop fusion | flops 3932160 | bytes 15728640 | tf_op jit(solution)/shard_map/concatenate | solution.py:100
  138.0 17.2 %while.10 = (s32[]{:T(128)}, bf16[2,30,128,128]{2,3,1,0:T(8,128)(2,1)}, s32[2,512]{1,0:T(2,128)S(1)}, s32[2,30,512]{2,1,0:T(8,128)S(1)}, bf16[2,30,512,128]{3,2,...) while((s32[]{:T(128)}, bf16[2,30,128,128]{2,3,1,0:T(8,128)(2,1)}, s32[2,512]{1,0:T(2,128)S(1)}, ...), condition=%wide.region_1.2_spmd, body=%wide.region_0.0_spmd.sunk | while | flops 2526904320 | bytes 5242453 | solution.py:111
  138.0 8.6 %fusion.88 = bf16[2,30,128,128]{2,3,1,0:T(8,128)(2,1)} fusion(bf16[2,30,128,128]{2,3,1,0:T(8,128)(2,1)} %get-tuple-element.100, s32[]{:T(128)} %get-tuple-element.99, bf16[2,30,512,128]{3,2,1,0:T(8,128)(2,1)} %get-tuple-element.110, s32[30,512]{1,0:T(8,128)S(1)} %dynamic-slice_bitcast_fusion.4, s32[512]{0:T(512)S(1)} %bitcast.150, ...), kind=kOutput, calls=%fused_computation.20.clone.1 | convolution fusion | flops 2526904320 | bytes 5115392 | tf_op jit(solution)/shard_map/while/body/eval_jaxpr/ua,sub->sab/dot_general | solution.py:32
  146.6 8.5 %fusion.88 = bf16[2,30,128,128]{2,3,1,0:T(8,128)(2,1)} fusion(bf16[2,30,128,128]{2,3,1,0:T(8,128)(2,1)} %get-tuple-element.100, s32[]{:T(128)} %get-tuple-element.99, bf16[2,30,512,128]{3,2,1,0:T(8,128)(2,1)} %get-tuple-element.110, s32[30,512]{1,0:T(8,128)S(1)} %dynamic-slice_bitcast_fusion.4, s32[512]{0:T(512)S(1)} %bitcast.150, ...), kind=kOutput, calls=%fused_computation.20.clone.1 | convolution fusion | flops 2526904320 | bytes 5115392 | tf_op jit(solution)/shard_map/while/body/eval_jaxpr/ua,sub->sab/dot_general | solution.py:32
  155.2 3.6 %multiply_reduce_fusion.1 = f32[2,128,128]{2,1,0:T(8,128)S(1)} fusion(bf16[2,30,128,128]{2,3,1,0:T(8,128)(2,1)} %get-tuple-element.34, f32[2,30]{1,0:T(2,128)S(1)} %pad_maximum_fusion.1, bf16[2,24,128,128]{3,2,1,0:T(8,128)(2,1)S(1)} %bitcast.138, bf16[2,6,128,128]{3,2,1,0:T(8,128)(2,1)} %bitcast.147), kind=kOutput, calls=%fused_computation.28 | convolution fusion | flops 507215872 | bytes 4063472 | tf_op jit(solution)/shard_map/psac,psdc->psad/dot_general | solution.py:123
  158.9 0.8 fusion.72
  159.7 1.7 broadcast_in_dim.73
  161.4 6.7 %all-to-all-start.2 = ((bf16[8,1,2,128,128]{4,3,2,1,0:T(8,128)(2,1)}), bf16[8,1,2,128,128]{4,3,2,1,0:T(8,128)(2,1)S(1)}, u32[]{:S(2)}, u32[]{:S(2)}) async-start(bf16[8,1,2,128,128]{4,3,2,1,0:T(8,128)(2,1)} %broadcast_in_dim.73), calls=%async_computation.2 | async-start | bytes 1048576 | tf_op jit(solution)/shard_map/all_to_all | solution.py:12
  168.1 0.1 copy.35
  168.2 17.9 %all-to-all-done.2 = bf16[8,1,2,128,128]{4,3,2,1,0:T(8,128)(2,1)S(1)} async-done(((bf16[8,1,2,128,128]{4,3,2,1,0:T(8,128)(2,1)}), bf16[8,1,2,128,128]{4,3,2,1,0:T(8,128)(2,1)S(1)}, u32[]{:S(2)}, u32[]{:S(2)}) %all-to-all-start.2) | async-done | bytes 524320 | tf_op jit(solution)/shard_map/all_to_all | solution.py:12
  186.1 0.6 gather_fusion.6
  186.7 21.3 %all-gather.8.cloned.1.call-done = bf16[1,64,128,128]{3,2,0,1:T(8,128)(2,1)} async-done(((bf16[1,2,128,128]{3,2,0,1:T(8,128)(2,1)}), bf16[1,64,128,128]{3,2,0,1:T(8,128)(2,1)}) %all-gather.8.cloned.1.call-update) | async-done | bytes 2097168 | tf_op jit(solution)/shard_map/all_gather | solution.py:116
  208.0 2.4 %gather_fusion.7 = bf16[48,128,128]{2,1,0:T(8,128)(2,1)S(1)} fusion(bf16[64,128,128]{2,1,0:T(8,128)(2,1)} %bitcast.141, s32[1024]{0:T(1024)S(1)} %pad_clamp_fusion), kind=kCustom, calls=%fused_computation.7 | custom fusion | bytes 3145920 | tf_op jit(solution)/shard_map/gather | solution.py:100
  210.5 4.1 %multiply_reduce_fusion = f32[2,128,128]{2,1,0:T(8,128)} fusion(bf16[2,30,128,128]{2,3,1,0:T(8,128)(2,1)} %get-tuple-element.34, f32[2,30]{1,0:T(2,128)S(1)} %pad_maximum_fusion.1, bf16[2,24,128,128]{3,2,1,0:T(8,128)(2,1)S(1)} %bitcast.139, bf16[2,6,128,128]{3,2,1,0:T(8,128)(2,1)S(1)} %bitcast.148), kind=kOutput, calls=%fused_computation.27 | convolution fusion | flops 507215872 | bytes 4063472 | tf_op jit(solution)/shard_map/psac,psdc->psad/dot_general | solution.py:123
  214.6 1.0 fusion.62
  215.7 0.1 copy.34
  215.8 0.6 fusion.60
  (43 shorter events, 0.2 us)
Async XLA Ops:
  7.2 34.2 %copy-start = (s32[8,64,512]{2,1,0:T(8,128)S(1)}, s32[8,64,512]{2,1,0:T(8,128)}, u32[]{:S(2)}) copy-start(s32[8,64,512]{2,1,0:T(8,128)} %param.16) | copy-start | bytes 3145732
  7.2 28.5 %copy-start.7 = (bf16[1,2,512,128]{3,2,1,0:T(8,128)(2,1)S(1)}, bf16[1,2,512,128]{3,2,1,0:T(8,128)(2,1)}, u32[]{:S(2)}) copy-start(bf16[1,2,512,128]{3,2,1,0:T(8,128)(2,1)} %param.15) | copy-start | bytes 786436
  7.2 87.5 %all-gather.6.cloned.1.call-start = ((), (), s32[]{:S(2)}) async-start(), calls=%async_computation.4 | async-start | bytes 2162688 | tf_op jit(solution)/shard_map/all_gather | solution.py:116
  8.9 114.0 %all-gather.4.cloned.1.call-start = ((), (), s32[]{:S(2)}) async-start(), calls=%async_computation.3 | async-start | bytes 8650752 | tf_op jit(solution)/shard_map/all_gather | solution.py:109
  37.4 3.8 %copy-start.10 = (s32[1,2,24]{2,1,0:T(2,128)S(1)}, s32[1,2,24]{2,1,0:T(2,128)}, u32[]{:S(2)}) copy-start(s32[1,2,24]{2,1,0:T(2,128)} %param.25) | copy-start | bytes 580
  37.4 4.0 %copy-start.9 = (s32[1,2,6]{2,1,0:T(2,128)S(1)}, s32[1,2,6]{2,1,0:T(2,128)}, u32[]{:S(2)}) copy-start(s32[1,2,6]{2,1,0:T(2,128)} %param.24) | copy-start | bytes 148
  37.4 5.4 %copy-start.12 = (f32[1,8]{1,0:T(1,128)S(1)}, f32[1,8]{1,0:T(1,128)}, u32[]{:S(2)}) copy-start(f32[1,8]{1,0:T(1,128)} %param.22) | copy-start | bytes 100
  37.4 6.8 %copy-start.1 = (f32[64,2]{0,1:T(2,128)S(1)}, f32[64,2]{0,1:T(2,128)}, u32[]{:S(2)}) copy-start(f32[64,2]{0,1:T(2,128)} %param.23) | copy-start | bytes 1540
  37.4 55.3 %all-to-all-start = ((bf16[8,1,2,512,128]{4,3,2,1,0:T(8,128)(2,1)}), bf16[8,1,2,512,128]{4,3,2,1,0:T(8,128)(2,1)S(1)}, u32[]{:S(2)}, u32[]{:S(2)}) async-start(bf16[8,1,2,512,128]{4,3,2,1,0:T(8,128)(2,1)} %broadcast_in_dim.43), calls=%async_computation | async-start | bytes 4194304 | tf_op jit(solution)/shard_map/all_to_all | solution.py:12
  41.2 166.8 %all-gather.8.cloned.1.call-start = ((), (), s32[]{:S(2)}) async-start(), calls=%async_computation.5 | async-start | bytes 2162688 | tf_op jit(solution)/shard_map/all_gather | solution.py:116
  122.9 8.5 %copy-start.2 = (bf16[12,512,128]{2,1,0:T(8,128)(2,1)S(1)}, bf16[12,512,128]{2,1,0:T(8,128)(2,1)}, u32[]{:S(2)}) copy-start(bf16[12,512,128]{2,1,0:T(8,128)(2,1)} %gather_fusion.2) | copy-start | bytes 4718596
  138.0 17.2 %copy-start.3 = (bf16[48,128,128]{2,1,0:T(8,128)(2,1)S(1)}, bf16[48,128,128]{2,1,0:T(8,128)(2,1)}, u32[]{:S(2)}) copy-start(bf16[48,128,128]{2,1,0:T(8,128)(2,1)} %gather_fusion.5) | copy-start | bytes 4718596
  155.1 3.7 %copy-start.4 = (f32[1,2,128,128]{3,2,1,0:T(8,128)S(1)}, f32[1,2,128,128]{3,2,1,0:T(8,128)}, u32[]{:S(2)}) copy-start(f32[1,2,128,128]{3,2,1,0:T(8,128)} %param.17) | copy-start | bytes 393220
  155.1 3.7 %copy-start.6 = (f32[1,2,128,128]{3,2,1,0:T(8,128)S(1)}, f32[1,2,128,128]{3,2,1,0:T(8,128)}, u32[]{:S(2)}) copy-start(f32[1,2,128,128]{3,2,1,0:T(8,128)} %param.18) | copy-start | bytes 393220
  155.1 3.7 %copy-start.8 = (f32[1,2,128]{2,1,0:T(2,128)S(1)}, f32[1,2,128]{2,1,0:T(2,128)}, u32[]{:S(2)}) copy-start(f32[1,2,128]{2,1,0:T(2,128)} %param.19) | copy-start | bytes 3076
  155.1 3.7 %copy-start.11 = (f32[2]{0:T(128)S(1)}, f32[2]{0:T(128)}, u32[]{:S(2)}) copy-start(f32[2]{0:T(128)} %param.21) | copy-start | bytes 28
  161.4 24.7 %all-to-all-start.2 = ((bf16[8,1,2,128,128]{4,3,2,1,0:T(8,128)(2,1)}), bf16[8,1,2,128,128]{4,3,2,1,0:T(8,128)(2,1)S(1)}, u32[]{:S(2)}, u32[]{:S(2)}) async-start(bf16[8,1,2,128,128]{4,3,2,1,0:T(8,128)(2,1)} %broadcast_in_dim.73), calls=%async_computation.2 | async-start | bytes 1048576 | tf_op jit(solution)/shard_map/all_to_all | solution.py:12
  215.7 0.7 copy-start.5
Sparse Core Ops, SparseCore 0:
  10.6 52.7 all-gather.5
  65.9 56.9 all-gather.3
  159.8 48.2 all-gather.7
where the time goes:
time: 224 us; the launch traced here: 223 us
  waiting for transfers between devices  105 us (47%)
  local copies, waits for them, and re-layouts  29.2 us (13%)
  blocking collectives  25 us (11%)
  matrix products  24.9 us (11%)
  between operations  14.6 us (7%)
  other arithmetic  14 us (6%)
  starting transfers between devices  10.6 us (5%)
    all_to_all x2, waiting for transfers between devices, sent_to_all(): return lax.all_to_all(copies, axis, split_axis=0, concat_axis=0, tiled=True)  57.9 us
    all_to_all x1, blocking collectives, sent_to_all(): return lax.all_to_all(copies, axis, split_axis=0, concat_axis=0, tiled=True)  25 us
    all_gather x1, waiting for transfers between devices, local(): row_bases = lax.all_gather(pno_basis, 'ja', axis=1, tiled=True)  24.7 us
    all_gather x2, waiting for transfers between devices, local(): row_rounded = lax.all_gather(rounded, 'ja', axis=1, tiled=True)  21.3 us
    dot_general x2, matrix products, pair_intersections(): jnp.einsum('ua,sub->sab', own_basis, picked, preferred_element_type=jnp.f...  17.1 us
    gather x3, local copies, waits for them, and re-layouts, slot_pick(): row_flat[column_slots]  14.5 us
    all_to_all x2, starting transfers between devices, sent_to_all(): return lax.all_to_all(copies, axis, split_axis=0, concat_axis=0, tiled=True)  10.5 us
    dot_general x2, matrix products, local(): jnp.einsum('psac,psdc->psad', halved.astype(jnp.float32), intersection_wide)  7.79 us
  transfers between devices with their start and end apart: 5, of which 4 were waited for; matrix products, arithmetic and copies ran while one was open for 10% of the time, Pallas kernels for 0%

commit v1 on v0

--- a/solution.py
+++ b/solution.py
@@ -113,7 +113,10 @@
     for iteration in range(ITERS):
         rounded = current.astype(jnp.bfloat16)
         column_rounded = gathered_copies(rounded, "ia", 0)
-        row_rounded = lax.all_gather(rounded, "ja", axis=1, tiled=True)
+        size = lax.axis_size("ja")
+        pieces = jnp.stack([rounded for _ in range(size)])
+        pieces = lax.all_to_all(pieces, "ja", split_axis=0, concat_axis=0)
+        row_rounded = jnp.concatenate(pieces, axis=1)
         intersection_wide = stored.astype(jnp.float32)
         halved = jnp.einsum(
             "psab,psbc->psac",

time: 224 us -> 253 us (1.13)
  blocking collectives: 25 us -> 96.8 us
  waiting for transfers between devices: 105 us -> 59.3 us
  starting transfers between devices: 10.6 us -> 13.9 us
  other arithmetic: 14 us -> 11.4 us
    all_to_all x0 -> x1, blocking collectives: none -> 52.4 us  [local(): pieces = lax.all_to_all(pieces, 'ja', split_axis=0, concat_axis=0)]
    all_to_all x0 -> x1, waiting for transfers between devices: none -> 26.1 us  [local(): pieces = lax.all_to_all(pieces, 'ja', split_axis=0, concat_axis=0)]
    all_to_all x2 -> x1, waiting for transfers between devices: 57.9 us -> 32.5 us  [sent_to_all(): return lax.all_to_all(copies, axis, split_axis=0, concat_axis=0, tiled=True)]
    all_gather x1, waiting for transfers between devices: 24.7 us -> 0.01 us  [local(): row_bases = lax.all_gather(pno_basis, 'ja', axis=1, tiled=True)]
    all_gather x2 -> x0, waiting for transfers between devices: 21.3 us -> none  [local(): row_rounded = lax.all_gather(rounded, 'ja', axis=1, tiled=True)]
    all_to_all x1 -> x2, blocking collectives: 25 us -> 44.4 us  [sent_to_all(): return lax.all_to_all(copies, axis, split_axis=0, concat_axis=0, tiled=True)]
    all_to_all x0 -> x1, starting transfers between devices: none -> 10.1 us  [local(): pieces = lax.all_to_all(pieces, 'ja', split_axis=0, concat_axis=0)]
    all_to_all x2 -> x1, starting transfers between devices: 10.5 us -> 3.75 us  [sent_to_all(): return lax.all_to_all(copies, axis, split_axis=0, concat_axis=0, tiled=True)]
  transfers between devices with their start and end apart: 5 -> 3, of which waited for: 4 -> 2; matrix products, arithmetic and copies ran while one was open for 10% -> 9% of each run, Pallas kernels for 0% -> 0%
where the time goes in v1:
time: 253 us; the launch traced here: 252 us
  blocking collectives  96.8 us (38%)
  waiting for transfers between devices  59.3 us (23%)
  local copies, waits for them, and re-layouts  31.3 us (12%)
  matrix products  24.9 us (10%)
  between operations  15 us (6%)
  starting transfers between devices  13.9 us (5%)
  other arithmetic  11.4 us (5%)
    all_to_all x1, blocking collectives, local(): pieces = lax.all_to_all(pieces, 'ja', split_axis=0, concat_axis=0)  52.4 us
    all_to_all x2, blocking collectives, sent_to_all(): return lax.all_to_all(copies, axis, split_axis=0, concat_axis=0, tiled=True)  44.4 us
    all_to_all x1, waiting for transfers between devices, sent_to_all(): return lax.all_to_all(copies, axis, split_axis=0, concat_axis=0, tiled=True)  32.5 us
    all_to_all x1, waiting for transfers between devices, local(): pieces = lax.all_to_all(pieces, 'ja', split_axis=0, concat_axis=0)  26.1 us
    dot_general x2, matrix products, pair_intersections(): jnp.einsum('ua,sub->sab', own_basis, picked, preferred_element_type=jnp.f...  17.1 us
    gather x3, local copies, waits for them, and re-layouts, slot_pick(): row_flat[column_slots]  14 us
    all_to_all x1, starting transfers between devices, local(): pieces = lax.all_to_all(pieces, 'ja', split_axis=0, concat_axis=0)  10.1 us
    dot_general x2, matrix products, local(): jnp.einsum('psac,psdc->psad', halved.astype(jnp.float32), intersection_wide)  7.75 us
  transfers between devices with their start and end apart: 3, of which 2 were waited for; matrix products, arithmetic and copies ran while one was open for 9% of the time, Pallas kernels for 0%

profile of v1, /device:TPU:1, one launch (start us, length us, event | category | flops | bytes accessed | tf_op | source)
XLA Modules:
  0.0 252.5 jit_solution(17118645493353227879)
XLA Ops:
  7.2 0.0 copy-start
  7.2 0.0 all-gather.2.cloned.1.call-start
  7.2 0.7 all-gather.2.cloned.1.call-update
  7.9 0.9 convert_bitcast_fusion.1
  8.8 0.1 broadcast_in_dim.72
  8.9 25.0 %all_to_all.25 = bf16[8,1,2,128,128]{4,3,2,1,0:T(8,128)(2,1)} all-to-all(bf16[8,1,2,128,128]{4,3,2,1,0:T(8,128)(2,1)S(1)} %broadcast_in_dim.72), channel_id=1, replica_groups=mesh['ia'=8,'ja'=32] {'ia'}, dimensions={0} | all-to-all | bytes 1048576 | tf_op jit(solution)/shard_map/all_to_all | solution.py:12
  34.0 0.5 stack.4
  34.5 52.4 %all_to_all.26 = bf16[32,1,2,128,128]{4,3,2,1,0:T(8,128)(2,1)} all-to-all(bf16[32,1,2,128,128]{4,3,2,1,0:T(8,128)(2,1)S(1)} %stack.4), channel_id=1, replica_groups=mesh['ia'=8,'ja'=32] {'ja'}, dimensions={0} | all-to-all | bytes 4194304 | tf_op jit(solution)/shard_map/all_to_all | solution.py:118
  86.9 1.8 broadcast_in_dim.43
  88.7 3.7 %all-to-all-start = ((bf16[8,1,2,512,128]{4,3,2,1,0:T(8,128)(2,1)}), bf16[8,1,2,512,128]{4,3,2,1,0:T(8,128)(2,1)S(1)}, u32[]{:S(2)}, u32[]{:S(2)}) async-start(bf16[8,1,2,512,128]{4,3,2,1,0:T(8,128)(2,1)} %broadcast_in_dim.43), calls=%async_computation | async-start | bytes 4194304 | tf_op jit(solution)/shard_map/all_to_all | solution.py:12
  92.5 0.1 reshape.279
  92.7 0.1 reshape.271
  92.8 0.6 gather_fusion
  93.3 0.6 reshape.270
  93.9 0.1 reshape.335
  94.0 0.7 gather_fusion.8
  94.7 0.7 reshape.334
  95.4 0.1 reshape.343
  95.5 1.1 gather_fusion.9
  96.6 0.7 reshape.342
  97.9 1.3 gather_fusion.1
  99.2 0.7 fusion.66
  99.9 0.7 fusion.67
  100.6 0.6 pad_maximum_fusion.1
  101.3 0.9 pad_add_fusion
  102.2 2.4 gather_fusion.4
  104.6 3.5 %gather_fusion.5 = bf16[48,128,128]{2,1,0:T(8,128)(2,1)} fusion(bf16[64,128,128]{2,1,0:T(8,128)(2,1)} %bitcast.114, s32[1024]{0:T(1024)S(1)} %pad_clamp_fusion), kind=kCustom, calls=%fused_computation.5 | custom fusion | bytes 3145920 | tf_op jit(solution)/shard_map/gather | solution.py:100
  108.1 32.5 %all-to-all-done = bf16[8,1,2,512,128]{4,3,2,1,0:T(8,128)(2,1)S(1)} async-done(((bf16[8,1,2,512,128]{4,3,2,1,0:T(8,128)(2,1)}), bf16[8,1,2,512,128]{4,3,2,1,0:T(8,128)(2,1)S(1)}, u32[]{:S(2)}, u32[]{:S(2)}) %all-to-all-start) | async-done | bytes 2097184 | tf_op jit(solution)/shard_map/all_to_all | solution.py:12
  140.6 1.9 gather_fusion.2
  142.6 8.5 %gather_fusion.3 = bf16[48,512,128]{2,1,0:T(8,128)(2,1)} fusion(bf16[64,512,128]{2,1,0:T(8,128)(2,1)} %bitcast.117, s32[1024]{0:T(1024)S(1)} %pad_clamp_fusion), kind=kCustom, calls=%fused_computation.3 | custom fusion | bytes 12583104 | tf_op jit(solution)/shard_map/gather | solution.py:100
  151.1 6.5 %pad_maximum_fusion = bf16[2,30,512,128]{3,2,1,0:T(8,128)(2,1)} fusion(bf16[2,24,512,128]{3,2,1,0:T(8,128)(2,1)} %bitcast.112, bf16[2,6,512,128]{3,2,1,0:T(8,128)(2,1)S(1)} %bitcast.116), kind=kLoop, calls=%fused_computation.26 | loop fusion | flops 3932160 | bytes 15728640 | tf_op jit(solution)/shard_map/concatenate | solution.py:100
  157.6 17.2 %while.10 = (s32[]{:T(128)}, bf16[2,30,128,128]{2,3,1,0:T(8,128)(2,1)}, s32[2,512]{1,0:T(2,128)S(1)}, s32[2,30,512]{2,1,0:T(8,128)S(1)}, bf16[2,30,512,128]{3,2,...) while((s32[]{:T(128)}, bf16[2,30,128,128]{2,3,1,0:T(8,128)(2,1)}, s32[2,512]{1,0:T(2,128)S(1)}, ...), condition=%wide.region_1.2_spmd, body=%wide.region_0.0_spmd.sunk | while | flops 2526904320 | bytes 5242453 | solution.py:111
  157.6 8.6 %fusion.86 = bf16[2,30,128,128]{2,3,1,0:T(8,128)(2,1)} fusion(bf16[2,30,128,128]{2,3,1,0:T(8,128)(2,1)} %get-tuple-element.98, s32[]{:T(128)} %get-tuple-element.97, bf16[2,30,512,128]{3,2,1,0:T(8,128)(2,1)} %get-tuple-element.108, s32[30,512]{1,0:T(8,128)S(1)} %dynamic-slice_bitcast_fusion.4, s32[512]{0:T(512)S(1)} %bitcast.128, ...), kind=kOutput, calls=%fused_computation.20.clone.1 | convolution fusion | flops 2526904320 | bytes 5115392 | tf_op jit(solution)/shard_map/while/body/eval_jaxpr/ua,sub->sab/dot_general | solution.py:32
  166.3 8.5 %fusion.86 = bf16[2,30,128,128]{2,3,1,0:T(8,128)(2,1)} fusion(bf16[2,30,128,128]{2,3,1,0:T(8,128)(2,1)} %get-tuple-element.98, s32[]{:T(128)} %get-tuple-element.97, bf16[2,30,512,128]{3,2,1,0:T(8,128)(2,1)} %get-tuple-element.108, s32[30,512]{1,0:T(8,128)S(1)} %dynamic-slice_bitcast_fusion.4, s32[512]{0:T(512)S(1)} %bitcast.128, ...), kind=kOutput, calls=%fused_computation.20.clone.1 | convolution fusion | flops 2526904320 | bytes 5115392 | tf_op jit(solution)/shard_map/while/body/eval_jaxpr/ua,sub->sab/dot_general | solution.py:32
  174.8 3.7 %multiply_reduce_fusion.1 = f32[2,128,128]{2,1,0:T(8,128)S(1)} fusion(bf16[2,30,128,128]{2,3,1,0:T(8,128)(2,1)} %get-tuple-element.34, f32[2,30]{1,0:T(2,128)S(1)} %copy-done.12, bf16[2,24,128,128]{3,2,1,0:T(8,128)(2,1)S(1)} %bitcast.120, bf16[2,6,128,128]{3,2,1,0:T(8,128)(2,1)} %bitcast.125), kind=kOutput, calls=%fused_computation.28 | convolution fusion | flops 507215872 | bytes 4063472 | tf_op jit(solution)/shard_map/psac,psdc->psad/dot_general | solution.py:126
  178.5 0.1 convert_bitcast_fusion
  178.7 0.1 broadcast_in_dim.73
  178.8 19.4 %all_to_all.27 = bf16[8,1,2,128,128]{4,3,2,1,0:T(8,128)(2,1)} all-to-all(bf16[8,1,2,128,128]{4,3,2,1,0:T(8,128)(2,1)S(1)} %broadcast_in_dim.73), channel_id=1, replica_groups=mesh['ia'=8,'ja'=32] {'ia'}, dimensions={0} | all-to-all | bytes 1048576 | tf_op jit(solution)/shard_map/all_to_all | solution.py:12
  198.1 1.9 stack.5
  200.0 10.1 %all-to-all-start.4 = ((bf16[32,1,2,128,128]{4,3,2,1,0:T(8,128)(2,1)}), bf16[32,1,2,128,128]{4,3,2,1,0:T(8,128)(2,1)S(1)}, u32[]{:S(2)}, u32[]{:S(2)}) async-start(bf16[32,1,2,128,128]{4,3,2,1,0:T(8,128)(2,1)} %stack.5), calls=%async_computation.4 | async-start | bytes 4194304 | tf_op jit(solution)/shard_map/all_to_all | solution.py:118
  210.1 0.1 copy.30
  210.2 2.4 gather_fusion.6
  212.6 26.1 %all-to-all-done.4 = bf16[32,1,2,128,128]{4,3,2,1,0:T(8,128)(2,1)S(1)} async-done(((bf16[32,1,2,128,128]{4,3,2,1,0:T(8,128)(2,1)}), bf16[32,1,2,128,128]{4,3,2,1,0:T(8,128)(2,1)S(1)}, u32[]{:S(2)}, u32[]{:S(2)}) %all-to-all-start.4) | async-done | bytes 2097184 | tf_op jit(solution)/shard_map/all_to_all | solution.py:118
  238.7 2.0 gather_fusion.7
  240.7 4.1 %multiply_reduce_fusion = f32[2,128,128]{2,1,0:T(8,128)S(1)} fusion(bf16[2,30,128,128]{2,3,1,0:T(8,128)(2,1)} %get-tuple-element.34, f32[2,30]{1,0:T(2,128)S(1)} %copy-done.13, bf16[2,24,128,128]{3,2,1,0:T(8,128)(2,1)} %bitcast.121, bf16[2,6,128,128]{3,2,1,0:T(8,128)(2,1)} %bitcast.126), kind=kOutput, calls=%fused_computation.27 | convolution fusion | flops 507215872 | bytes 4063472 | tf_op jit(solution)/shard_map/psac,psdc->psad/dot_general | solution.py:126
  244.7 0.1 fusion.62
  244.9 0.1 copy.29
  245.0 0.6 fusion.60
  (44 shorter events, 0.2 us)
Async XLA Ops:
  7.2 85.4 %copy-start = (s32[8,64,512]{2,1,0:T(8,128)S(1)}, s32[8,64,512]{2,1,0:T(8,128)}, u32[]{:S(2)}) copy-start(s32[8,64,512]{2,1,0:T(8,128)} %param.16) | copy-start | bytes 3145732
  7.2 135.4 %all-gather.2.cloned.1.call-start = ((), (), s32[]{:S(2)}) async-start(), calls=%async_computation.5 | async-start | bytes 8650752 | tf_op jit(solution)/shard_map/all_gather | solution.py:109
  34.5 52.4 %copy-start.6 = (bf16[1,2,512,128]{3,2,1,0:T(8,128)(2,1)S(1)}, bf16[1,2,512,128]{3,2,1,0:T(8,128)(2,1)}, u32[]{:S(2)}) copy-start(bf16[1,2,512,128]{3,2,1,0:T(8,128)(2,1)} %param.15) | copy-start | bytes 786436
  88.7 3.8 %copy-start.10 = (s32[1,2,24]{2,1,0:T(2,128)S(1)}, s32[1,2,24]{2,1,0:T(2,128)}, u32[]{:S(2)}) copy-start(s32[1,2,24]{2,1,0:T(2,128)} %param.25) | copy-start | bytes 580
  88.7 3.9 %copy-start.9 = (s32[1,2,6]{2,1,0:T(2,128)S(1)}, s32[1,2,6]{2,1,0:T(2,128)}, u32[]{:S(2)}) copy-start(s32[1,2,6]{2,1,0:T(2,128)} %param.24) | copy-start | bytes 148
  88.7 5.3 %copy-start.14 = (f32[1,8]{1,0:T(1,128)S(1)}, f32[1,8]{1,0:T(1,128)}, u32[]{:S(2)}) copy-start(f32[1,8]{1,0:T(1,128)} %param.22) | copy-start | bytes 100
  88.7 6.8 %copy-start.1 = (f32[64,2]{0,1:T(2,128)S(1)}, f32[64,2]{0,1:T(2,128)}, u32[]{:S(2)}) copy-start(f32[64,2]{0,1:T(2,128)} %param.23) | copy-start | bytes 1540
  88.7 51.9 %all-to-all-start = ((bf16[8,1,2,512,128]{4,3,2,1,0:T(8,128)(2,1)}), bf16[8,1,2,512,128]{4,3,2,1,0:T(8,128)(2,1)S(1)}, u32[]{:S(2)}, u32[]{:S(2)}) async-start(bf16[8,1,2,512,128]{4,3,2,1,0:T(8,128)(2,1)} %broadcast_in_dim.43), calls=%async_computation | async-start | bytes 4194304 | tf_op jit(solution)/shard_map/all_to_all | solution.py:12
  142.6 8.5 %copy-start.2 = (bf16[12,512,128]{2,1,0:T(8,128)(2,1)S(1)}, bf16[12,512,128]{2,1,0:T(8,128)(2,1)}, u32[]{:S(2)}) copy-start(bf16[12,512,128]{2,1,0:T(8,128)(2,1)} %gather_fusion.2) | copy-start | bytes 4718596
  157.6 17.2 %copy-start.3 = (bf16[48,128,128]{2,1,0:T(8,128)(2,1)S(1)}, bf16[48,128,128]{2,1,0:T(8,128)(2,1)}, u32[]{:S(2)}) copy-start(bf16[48,128,128]{2,1,0:T(8,128)(2,1)} %gather_fusion.5) | copy-start | bytes 4718596
  157.6 17.2 %copy-start.12 = (f32[2,30]{1,0:T(2,128)S(1)}, f32[2,30]{1,0:T(2,128)}, u32[]{:S(2)}) copy-start(f32[2,30]{1,0:T(2,128)} %pad_maximum_fusion.1) | copy-start | bytes 724
  174.8 3.7 %copy-start.5 = (f32[1,2,128,128]{3,2,1,0:T(8,128)S(1)}, f32[1,2,128,128]{3,2,1,0:T(8,128)}, u32[]{:S(2)}) copy-start(f32[1,2,128,128]{3,2,1,0:T(8,128)} %param.18) | copy-start | bytes 393220
  174.8 3.7 %copy-start.7 = (f32[1,2,128,128]{3,2,1,0:T(8,128)S(1)}, f32[1,2,128,128]{3,2,1,0:T(8,128)}, u32[]{:S(2)}) copy-start(f32[1,2,128,128]{3,2,1,0:T(8,128)} %param.17) | copy-start | bytes 393220
  174.8 3.7 %copy-start.8 = (f32[1,2,128]{2,1,0:T(2,128)S(1)}, f32[1,2,128]{2,1,0:T(2,128)}, u32[]{:S(2)}) copy-start(f32[1,2,128]{2,1,0:T(2,128)} %param.19) | copy-start | bytes 3076
  174.8 3.7 %copy-start.11 = (f32[2]{0:T(128)S(1)}, f32[2]{0:T(128)}, u32[]{:S(2)}) copy-start(f32[2]{0:T(128)} %param.21) | copy-start | bytes 28
  200.0 38.7 %all-to-all-start.4 = ((bf16[32,1,2,128,128]{4,3,2,1,0:T(8,128)(2,1)}), bf16[32,1,2,128,128]{4,3,2,1,0:T(8,128)(2,1)S(1)}, u32[]{:S(2)}, u32[]{:S(2)}) async-start(bf16[32,1,2,128,128]{4,3,2,1,0:T(8,128)(2,1)} %stack.5), calls=%async_computation.4 | async-start | bytes 4194304 | tf_op jit(solution)/shard_map/all_to_all | solution.py:118
  212.6 28.0 %copy-start.13 = (f32[2,30]{1,0:T(2,128)S(1)}, f32[2,30]{1,0:T(2,128)}, u32[]{:S(2)}) copy-start(f32[2,30]{1,0:T(2,128)} %pad_maximum_fusion.1) | copy-start | bytes 724
  244.9 0.7 copy-start.4
Sparse Core Ops, SparseCore 0:
  10.5 78.4 all-gather.1
